TPU v7x, 128 devices: a whole 4x4x4 slice. The times are simulated.
128 devices in a mesh: wide: 16 (over y_hi, z, core), narrow: 8 (over y_lo, x).
Axes of the slice: x: 4, y: 4 (y_hi: 2, y_lo: 2; y = y_hi * 2 + y_lo), z: 4, core: 2. Of those that a mesh axis runs over, the one named last changes fastest.
Arguments:
- inputs: bfloat16 [1, 4096, 4096], P(None, 'narrow', 'wide'), may hold values from -6 to 6
- out_cotangent: bfloat16 [1, 1, 4096, 14336], P(None, None, ('wide', 'narrow')), may hold values from -0.0014648438 to 0.0014648438
- sign_bits: int32 [1, 4096, 16384], P(None, 'wide', 'narrow'), may hold values 0 or 1
- row_pick: int32 [1, 8192], replicated, may hold values from 0 to 4095
- col_pick: int32 [1, 8192], replicated, may hold values from 0 to 16383
Outputs:
- sketch: float32 [1, 1, 8192], P(None, None, ('wide', 'narrow'))
All inputs are finite; a program needn't handle non-finite values. No bound on the sum of `sign_bits` on one device may be relied on, other than what follows from the above.
Results may differ from a plain program's by a relative error of at most 0.0003.
Values may be sent and summed in bfloat16 or wider, within the bound.
A program may use at most 128 MiB of HBM per device.

v0:
```python
import jax
import jax.numpy as jnp
from jax import lax
from jax.sharding import PartitionSpec as P


def hadamard(length):
    index = jnp.arange(length, dtype=jnp.int32)
    parity = jnp.zeros((length, length), jnp.int32)
    for bit_number in range(length.bit_length() - 1):
        parity = parity ^ index[:, None] >> bit_number & 1 & (index[None, :] >> bit_number & 1)
    return (1 - 2 * parity).astype(jnp.float32)


def transform_last(block):
    width_all = block.shape[-1]
    leading = block.ndim - 1
    factors = []
    remain = width_all
    while remain > 1:
        factor = min(128, remain)
        factors.append(factor)
        remain = remain // factor
    shaped = block.reshape(block.shape[:-1] + tuple(factors))
    for placed, factor in enumerate(factors):
        mixed = jnp.tensordot(
            shaped,
            hadamard(factor),
            axes=([leading + placed], [0]),
            precision=lax.Precision.HIGHEST,
        )
        shaped = jnp.moveaxis(mixed, -1, leading + placed)
    return shaped.reshape(block.shape)


def body(inputs, out_cotangent, sign_bits, row_pick, col_pick):
    wide_count = lax.axis_size("wide")
    narrow_count = lax.axis_size("narrow")
    row_local = inputs.shape[2]
    col_local = sign_bits.shape[2]
    hidden_all = out_cotangent.shape[3]
    padded_width = col_local * narrow_count
    whole_inputs = lax.all_gather(inputs, "narrow", axis=1, tiled=True)
    padded_cot = jnp.pad(out_cotangent, ((0, 0), (0, 0), (0, 0), (0, padded_width - hidden_all)))
    column_cot = lax.all_to_all(padded_cot, "narrow", split_axis=3, concat_axis=2, tiled=True)
    grads = jnp.einsum(
        "etr,metc->merc",
        whole_inputs,
        lax.all_gather(column_cot, "wide", axis=2, tiled=True),
        preferred_element_type=jnp.float32,
    )
    signs = (2 * sign_bits - 1).astype(jnp.float32)
    row_mix = hadamard(row_local)
    wide_index = lax.axis_index("wide")
    narrow_index = lax.axis_index("narrow")
    row_high = row_pick // row_local
    row_low = row_pick % row_local
    col_high = col_pick // col_local
    col_low = col_pick % col_local
    position = row_low * col_local + col_low
    block_len = row_local * col_local
    piece_len = block_len // (wide_count * narrow_count)
    signed = grads[:, 0] * signs
    rows_done = jnp.einsum("ij,mjc->mic", row_mix, signed, precision=lax.Precision.HIGHEST)
    local_done = transform_last(rows_done).reshape(signed.shape[0], block_len)
    pieces = local_done.reshape(signed.shape[0], wide_count * narrow_count, piece_len)
    received = lax.all_to_all(pieces, ("wide", "narrow"), split_axis=1, concat_axis=1, tiled=True)
    finished = jnp.einsum(
        "ts,msj->mtj",
        hadamard(wide_count * narrow_count),
        received,
        precision=lax.Precision.HIGHEST,
    )
    my_piece = wide_index * narrow_count + narrow_index
    target = row_high * narrow_count + col_high
    owned = position // piece_len == my_piece
    lookup = target * piece_len + position % piece_len
    picked = jnp.take_along_axis(finished.reshape(signed.shape[0], -1), lookup, axis=1)
    contributions = [jnp.where(owned, picked, jnp.float32(0.0))]
    stacked = jnp.stack(contributions)
    summed = lax.psum_scatter(stacked, ("wide", "narrow"), scatter_dimension=2, tiled=True)
    return summed / jnp.sqrt(jnp.float32(row_pick.shape[1]))


def solution(mesh):
    return jax.shard_map(
        body,
        mesh=mesh,
        in_specs=(
            P(None, "narrow", "wide"),
            P(None, None, ("wide", "narrow"), None),
            P(None, "wide", "narrow"),
            P(),
            P(),
        ),
        out_specs=P(None, None, ("wide", "narrow")),
        check_vma=False,
    )
```

profile of v0, /device:TPU:0, one launch (start us, length us, event | category | flops | bytes accessed | tf_op | source)
XLA Modules:
  0.0 1106.1 jit_solution(14091993724530731446)
XLA Ops:
  6.5 0.0 all-gather.5.cloned.1.call-start
  6.5 0.7 all-gather.5.cloned.1.call-update
  7.3 0.0 all-gather.3.cloned.1.call-start
  7.3 14.3 %copy.20 = bf16[1,1,32,14336]{2,1,0,3:T(2,128)(2,1)} copy(bf16[1,1,32,14336]{3,2,1,0:T(8,128)(2,1)} %param.6) | data formatting | bytes 1835008 | tf_op args[1]
  21.6 18.6 %pad_bitcast_fusion = bf16[16384,1,1,32]{3,2,1,0:T(2,128)(2,1)} fusion(bf16[1,1,32,14336]{2,1,0,3:T(2,128)(2,1)} %copy.20), kind=kLoop, calls=%fused_computation.160 | loop fusion | bytes 1966080
  40.2 0.5 broadcast.581
  40.7 90.8 %reduce = bf16[16384,32]{1,0:T(8,128)(2,1)} reduce(bf16[16384,1,1,32]{3,2,1,0:T(2,128)(2,1)} %pad_bitcast_fusion, bf16[]{:T(256)} %broadcast.581), dimensions={1,2}, to_apply=%pad_bitcast_fusion.reduce_sub_computation | reduce | bytes 2097154
  131.5 7.0 reshape.337
  138.4 20.9 %all_to_all.23 = bf16[8,2,32768]{2,1,0:T(2,128)(2,1)S(1)} all-to-all(bf16[8,2,32768]{2,1,0:T(2,128)(2,1)S(1)} %reshape.337), channel_id=1, replica_groups=mesh['wide'=16,'narrow'=8] {'narrow'}, dimensions={0} | all-to-all | bytes 2097152 | tf_op jit(solution)/shard_map/all_to_all | solution.py:45
  159.4 6.2 reshape.338
  165.6 15.1 %copy.21 = bf16[1,1,32,16384]{3,2,1,0:T(8,128)(2,1)S(1)} copy(bf16[1,1,32,16384]{2,1,0,3:T(2,128)(2,1)} %bitcast.73) | data formatting | bytes 2097152 | tf_op jit(solution)/shard_map/all_to_all | solution.py:45
  180.7 0.6 copy.33
  181.3 0.0 copy-start
  181.3 1.6 copy.22
  182.9 0.0 all-gather.3.cloned.1.call-update
  182.9 0.1 copy-done
  183.0 2.3 copy.23
  185.4 0.0 all-gather.5.cloned.1.call-done
  185.4 106.8 %all-gather.3.cloned.1.call-done = bf16[1,1,4096,2048]{3,2,1,0:T(8,128)(2,1)} async-done(((bf16[1,1,256,2048]{3,2,1,0:T(8,128)(2,1)}), bf16[1,1,4096,2048]{3,2,1,0:T(8,128)(2,1)}) %all-gather.3.cloned.1.call-update) | async-done | bytes 16777232 | tf_op jit(solution)/shard_map/all_gather | solution.py:49
  292.2 12.4 %fusion.8 = f32[256,2048]{0,1:T(8,128)S(1)} fusion(bf16[1,1,4096,2048]{3,2,1,0:T(8,128)(2,1)} %all-gather.3.cloned.1.call-done, bf16[1,4096,256]{2,1,0:T(8,128)(2,1)} %all-gather.5.cloned.1.call-done, s32[1,256,2048]{1,2,0:T(8,128)} %copy.23), kind=kOutput, calls=%fused_computation.6 | convolution fusion | flops 4297064448 | bytes 23068672 | tf_op jit(solution)/shard_map/etr,metc->merc/dot_general | solution.py:46
  304.6 2.2 fusion.21
  306.8 4.4 fusion.18
  311.2 29.0 %fusion.14 = f32[256,128,16]{2,1,0:T(8,128)} fusion(f32[256,128,16]{1,0,2:T(8,128)S(1)} %fusion.18, s32[16]{0:T(128)S(1)} %get-tuple-element.21, s32[16]{0:T(128)S(1)} %get-tuple-element.22, s32[16]{0:T(128)S(1)} %get-tuple-element.23, s32[16]{0:T(128)S(1)} %get-tuple-element.24), kind=kOutput, calls=%fused_computation.10 | convolution fusion | flops 100665856 | bytes 4194560 | tf_op jit(solution)/shard_map/dot_general | solution.py:26
  340.2 12.3 %reshape_reshape_reshape.4 = f32[1,128,4096]{2,0,1:T(1,128)} reshape(f32[256,128,16]{2,1,0:T(8,128)} %fusion.14) | data formatting | bytes 4194304 | tf_op jit(solution)/shard_map/reshape;reshape;reshape | solution.py:66
  352.5 0.0 copy-start.1
  352.5 0.0 copy-start.2
  352.5 6.2 all-to-all-start.1
  358.7 0.3 reduce-scatter.4.cloned.1.call-start
  359.0 0.0 copy-done.1
  359.0 0.0 copy-done.2
  359.0 0.6 compare_select_fusion
  359.7 29.0 %all-to-all-done.1 = f32[1,128,4096]{2,0,1:T(1,128)S(1)} async-done(((f32[1,128,4096]{2,0,1:T(1,128)}), f32[1,128,4096]{2,0,1:T(1,128)S(1)}, u32[]{:S(2)}, u32[]{:S(2)}) %all-to-all-start.1) | async-done | bytes 2097184 | tf_op jit(solution)/shard_map/all_to_all | solution.py:67
  388.7 5.7 convolution_bitcast_fusion
  394.3 2.9 copy.28
  397.3 2.0 copy.34
  399.2 45.5 %gather_fusion = f32[8192]{0:T(1024)S(1)} fusion(f32[524288]{0:T(1024)S(1)} %bitcast.72, s32[8192]{0:T(1024)S(1)} %broadcast_clamp_fusion), kind=kCustom, calls=%fused_computation | custom fusion | bytes 98304 | tf_op jit(solution)/shard_map/jit(take_along_axis)/gather | solution.py:78
  444.8 0.2 fusion.64
  445.0 6.3 copy.30
  451.3 0.0 reduce-scatter.4.cloned.1.call-update
  451.3 646.6 %reduce-scatter.4.cloned.1.call-done = f32[64,1]{1,0:T(8,128)} async-done(((f32[8192,1]{1,0:T(8,128)}), f32[64,1]{1,0:T(8,128)}) %reduce-scatter.4.cloned.1.call-update) | async-done | bytes 272
  1098.0 0.8 copy.31
  1098.8 0.5 broadcast_multiply_fusion
  (11 shorter events, 0.1 us)
Async XLA Ops:
  6.5 178.9 %all-gather.5.cloned.1.call-start = ((), (), s32[]{:S(2)}) async-start(), calls=%async_computation.4 | async-start | bytes 2359296 | tf_op jit(solution)/shard_map/all_gather | solution.py:43
  7.3 284.9 %all-gather.3.cloned.1.call-start = ((), (), s32[]{:S(2)}) async-start(), calls=%async_computation.3 | async-start | bytes 17825792 | tf_op jit(solution)/shard_map/all_gather | solution.py:49
  181.3 1.7 copy-start
  352.5 6.5 copy-start.1
  352.5 6.5 copy-start.2
  352.5 36.2 %all-to-all-start.1 = ((f32[1,128,4096]{2,0,1:T(1,128)}), f32[1,128,4096]{2,0,1:T(1,128)S(1)}, u32[]{:S(2)}, u32[]{:S(2)}) async-start(f32[1,128,4096]{2,0,1:T(1,128)} %reshape_reshape_reshape.4), calls=%async_computation.1 | async-start | bytes 4194304 | tf_op jit(solution)/shard_map/all_to_all | solution.py:67
  358.7 739.2 %reduce-scatter.4.cloned.1.call-start = ((), (), s32[]{:S(2)}) async-start(), calls=%async_computation.5 | async-start | bytes 4227072
Sparse Core Ops, SparseCore 0:
  9.0 43.6 all-gather.4
  183.0 109.0 all-gather.2
  451.5 646.4 reduce-scatter.3
where the time goes:
time: 1120 us; the launch traced here: 1110 us
  waiting for transfers between devices  783 us (70%)
  local copies, waits for them, and re-layouts  136 us (12%)
  other arithmetic  92.2 us (8%)
  matrix products  53.7 us (5%)
  blocking collectives  20.9 us (2%)
  between operations  13.5 us (1%)
    unnamed x4, waiting for transfers between devices  647 us
    all_gather x1, waiting for transfers between devices, body(): lax.all_gather(column_cot, 'wide', axis=2, tiled=True)  107 us
    unnamed x1, other arithmetic  90.8 us
    unnamed x16, local copies, waits for them, and re-layouts  58.7 us
    gather x1, local copies, waits for them, and re-layouts, body(): jnp.take_along_axis(finished.reshape(signed.shape[0], -1), lookup, axis=1)  45.5 us
    dot_general x2, matrix products, transform_last(): jnp.tensordot(shaped, hadamard(factor), axes=([leading + placed], [0]), p...  33.4 us
    all_to_all x1, waiting for transfers between devices, body(): lax.all_to_all(pieces, ('wide', 'narrow'), split_axis=1, concat_axis=1, t...  29 us
  transfers between devices with their start and end apart: 4, of which 3 were waited for; matrix products, arithmetic and copies ran while one was open for 14% of the time, Pallas kernels for 0%

commit v1 on v0

--- a/solution.py
+++ b/solution.py
@@ -2,6 +2,11 @@
 import jax.numpy as jnp
 from jax import lax
 from jax.sharding import PartitionSpec as P
+
+
+def all_by_exchange(x, name, dim):
+    sent = jnp.stack([x] * lax.axis_size(name))
+    return jnp.concatenate(lax.all_to_all(sent, name, 0, 0), axis=dim)
 
 
 def hadamard(length):
@@ -46,7 +51,7 @@
     grads = jnp.einsum(
         "etr,metc->merc",
         whole_inputs,
-        lax.all_gather(column_cot, "wide", axis=2, tiled=True),
+        all_by_exchange(column_cot, "wide", 2),
         preferred_element_type=jnp.float32,
     )
     signs = (2 * sign_bits - 1).astype(jnp.float32)

time: 1120 us -> 1300 us (1.16)
  waiting for transfers between devices: 783 us -> 934 us
  starting transfers between devices: 6.52 us -> 33.9 us
    all_to_all x0 -> x1, waiting for transfers between devices: none -> 217 us  [all_by_exchange(): return jnp.concatenate(lax.all_to_all(sent, name, 0, 0), axis=dim)]
    all_gather x1 -> x0, waiting for transfers between devices: 107 us -> none  [body(): lax.all_gather(column_cot, 'wide', axis=2, tiled=True)]
    all_gather x1, waiting for transfers between devices: 0.02 us -> 40.5 us  [body(): whole_inputs = lax.all_gather(inputs, 'narrow', axis=1, tiled=True)]
    all_to_all x1, starting transfers between devices: 6.23 us -> 25.6 us  [body(): lax.all_to_all(pieces, ('wide', 'narrow'), split_axis=1, concat_axis=1, t...]
    unnamed x4 -> x3, waiting for transfers between devices: 647 us -> 647 us
  transfers between devices with their start and end apart: 4 -> 4, of which waited for: 3 -> 4; matrix products, arithmetic and copies ran while one was open for 14% -> 0% of each run, Pallas kernels for 0% -> 0%
where the time goes in v1:
time: 1300 us; the launch traced here: 1290 us
  waiting for transfers between devices  934 us (72%)
  local copies, waits for them, and re-layouts  141 us (11%)
  other arithmetic  92.2 us (7%)
  matrix products  53.7 us (4%)
  starting transfers between devices  33.9 us (3%)
  blocking collectives  20.9 us (2%)
  between operations  13.8 us (1%)
    unnamed x3, waiting for transfers between devices  647 us
    all_to_all x1, waiting for transfers between devices, all_by_exchange(): return jnp.concatenate(lax.all_to_all(sent, name, 0, 0), axis=dim)  217 us
    unnamed x1, other arithmetic  90.8 us
    unnamed x16, local copies, waits for them, and re-layouts  58.6 us
    gather x1, local copies, waits for them, and re-layouts, body(): jnp.take_along_axis(finished.reshape(signed.shape[0], -1), lookup, axis=1)  45.5 us
    all_gather x1, waiting for transfers between devices, body(): whole_inputs = lax.all_gather(inputs, 'narrow', axis=1, tiled=True)  40.5 us
    dot_general x2, matrix products, transform_last(): jnp.tensordot(shaped, hadamard(factor), axes=([leading + placed], [0]), p...  33.4 us
    all_to_all x1, waiting for transfers between devices, body(): lax.all_to_all(pieces, ('wide', 'narrow'), split_axis=1, concat_axis=1, t...  29 us
  transfers between devices with their start and end apart: 4, of which 4 were waited for; matrix products, arithmetic and copies ran while one was open for 0% of the time, Pallas kernels for 0%

profile of v1, /device:TPU:0, one launch (start us, length us, event | category | flops | bytes accessed | tf_op | source)
XLA Modules:
  0.0 1289.5 jit_solution(13824541252869391909)
XLA Ops:
  6.5 14.3 %copy.20 = bf16[1,1,32,14336]{2,1,0,3:T(2,128)(2,1)} copy(bf16[1,1,32,14336]{3,2,1,0:T(8,128)(2,1)} %param.6) | data formatting | bytes 1835008 | tf_op args[1]
  20.8 18.6 %pad_bitcast_fusion = bf16[16384,1,1,32]{3,2,1,0:T(2,128)(2,1)} fusion(bf16[1,1,32,14336]{2,1,0,3:T(2,128)(2,1)} %copy.20), kind=kLoop, calls=%fused_computation.158 | loop fusion | bytes 1966080
  39.4 0.5 broadcast.583
  39.9 90.8 %reduce = bf16[16384,32]{1,0:T(8,128)(2,1)} reduce(bf16[16384,1,1,32]{3,2,1,0:T(2,128)(2,1)} %pad_bitcast_fusion, bf16[]{:T(256)} %broadcast.583), dimensions={1,2}, to_apply=%pad_bitcast_fusion.reduce_sub_computation | reduce | bytes 2097154
  130.7 7.0 reshape.344
  137.6 20.9 %all_to_all.25 = bf16[8,2,32768]{2,1,0:T(2,128)(2,1)S(1)} all-to-all(bf16[8,2,32768]{2,1,0:T(2,128)(2,1)S(1)} %reshape.344), channel_id=1, replica_groups=mesh['wide'=16,'narrow'=8] {'narrow'}, dimensions={0} | all-to-all | bytes 2097152 | tf_op jit(solution)/shard_map/all_to_all | solution.py:50
  158.6 6.2 reshape.345
  164.8 15.1 %copy.21 = bf16[1,1,32,16384]{3,2,1,0:T(8,128)(2,1)S(1)} copy(bf16[1,1,32,16384]{2,1,0,3:T(2,128)(2,1)} %bitcast.66) | data formatting | bytes 2097152 | tf_op jit(solution)/shard_map/all_to_all | solution.py:50
  179.9 0.6 copy.33
  180.5 0.6 copy.22
  181.1 6.0 stack.7
  187.1 0.0 copy-start
  187.1 7.9 all-to-all-start.1
  195.1 0.0 all-gather.2.cloned.1.call-start
  195.1 0.7 all-gather.2.cloned.1.call-update
  195.8 0.0 copy-done
  195.8 2.3 copy.23
  198.2 40.5 %all-gather.2.cloned.1.call-done = bf16[1,4096,256]{2,1,0:T(8,128)(2,1)} async-done(((bf16[1,512,256]{2,1,0:T(8,128)(2,1)}), bf16[1,4096,256]{2,1,0:T(8,128)(2,1)}) %all-gather.2.cloned.1.call-update) | async-done | bytes 2097168 | tf_op jit(solution)/shard_map/all_gather | solution.py:48
  238.7 217.1 %all-to-all-done.1 = bf16[16,1,1,256,2048]{4,3,2,1,0:T(8,128)(2,1)} async-done(((bf16[16,1,1,256,2048]{4,3,2,1,0:T(8,128)(2,1)}), bf16[16,1,1,256,2048]{4,3,2,1,0:T(8,128)(2,1)}, u32[]{:S(2)}, u32[]{:S(2)}) %all-to-all-start.1) | async-done | bytes 16777248 | tf_op jit(solution)/shard_map/all_to_all | solution.py:9
  455.8 12.4 fusion.1
  468.2 2.2 fusion.12
  470.4 4.4 fusion.9
  474.8 29.0 %fusion.5 = f32[256,128,16]{2,1,0:T(8,128)} fusion(f32[256,128,16]{1,0,2:T(8,128)S(1)} %fusion.9, s32[16]{0:T(128)S(1)} %get-tuple-element.21, s32[16]{0:T(128)S(1)} %get-tuple-element.22, s32[16]{0:T(128)S(1)} %get-tuple-element.23, s32[16]{0:T(128)S(1)} %get-tuple-element.24), kind=kOutput, calls=%fused_computation.8 | convolution fusion | flops 100665856 | bytes 4194560 | tf_op jit(solution)/shard_map/dot_general | solution.py:31
  503.8 12.3 reshape_reshape_reshape.4
  516.2 0.0 copy-start.1
  516.2 0.0 copy-start.2
  516.2 25.6 %all-to-all-start.2 = ((f32[1,128,4096]{2,0,1:T(1,128)}), f32[1,128,4096]{2,0,1:T(1,128)S(1)}, u32[]{:S(2)}, u32[]{:S(2)}) async-start(f32[1,128,4096]{2,0,1:T(1,128)} %reshape_reshape_reshape.4), calls=%async_computation.2 | async-start | bytes 4194304 | tf_op jit(solution)/shard_map/all_to_all | solution.py:72
  541.8 0.3 reduce-scatter.4.cloned.1.call-start
  542.1 0.0 copy-done.1
  542.1 0.0 copy-done.2
  542.1 0.6 compare_select_fusion
  542.7 29.0 %all-to-all-done.2 = f32[1,128,4096]{2,0,1:T(1,128)S(1)} async-done(((f32[1,128,4096]{2,0,1:T(1,128)}), f32[1,128,4096]{2,0,1:T(1,128)S(1)}, u32[]{:S(2)}, u32[]{:S(2)}) %all-to-all-start.2) | async-done | bytes 2097184 | tf_op jit(solution)/shard_map/all_to_all | solution.py:72
  571.7 5.7 convolution_bitcast_fusion
  577.4 2.9 copy.28
  580.3 2.0 copy.34
  582.3 45.5 %gather_fusion = f32[8192]{0:T(1024)S(1)} fusion(f32[524288]{0:T(1024)S(1)} %bitcast.65, s32[8192]{0:T(1024)S(1)} %broadcast_clamp_fusion), kind=kCustom, calls=%fused_computation | custom fusion | bytes 98304 | tf_op jit(solution)/shard_map/jit(take_along_axis)/gather | solution.py:83
  627.8 0.2 fusion.55
  628.0 6.3 copy.30
  634.4 0.0 reduce-scatter.4.cloned.1.call-update
  634.4 646.6 %reduce-scatter.4.cloned.1.call-done = f32[64,1]{1,0:T(8,128)} async-done(((f32[8192,1]{1,0:T(8,128)}), f32[64,1]{1,0:T(8,128)}) %reduce-scatter.4.cloned.1.call-update) | async-done | bytes 272
  1281.0 0.8 copy.31
  1281.9 0.5 broadcast_multiply_fusion
  (11 shorter events, 0.1 us)
Async XLA Ops:
  187.1 8.7 copy-start
  187.1 268.7 %all-to-all-start.1 = ((bf16[16,1,1,256,2048]{4,3,2,1,0:T(8,128)(2,1)}), bf16[16,1,1,256,2048]{4,3,2,1,0:T(8,128)(2,1)}, u32[]{:S(2)}, u32[]{:S(2)}) async-start(bf16[16,1,1,256,2048]{4,3,2,1,0:T(8,128)(2,1)} %stack.7), calls=%async_computation.1 | async-start | bytes 33554432 | tf_op jit(solution)/shard_map/all_to_all | solution.py:9
  195.1 43.7 %all-gather.2.cloned.1.call-start = ((), (), s32[]{:S(2)}) async-start(), calls=%async_computation.4 | async-start | bytes 2359296 | tf_op jit(solution)/shard_map/all_gather | solution.py:48
  516.2 25.9 %copy-start.1 = (s32[1,8192]{1,0:T(1,128)S(1)}, s32[1,8192]{1,0:T(1,128)}, u32[]{:S(2)}) copy-start(s32[1,8192]{1,0:T(1,128)} %param.9) | copy-start | bytes 98308
  516.2 25.9 %copy-start.2 = (s32[1,8192]{1,0:T(1,128)S(1)}, s32[1,8192]{1,0:T(1,128)}, u32[]{:S(2)}) copy-start(s32[1,8192]{1,0:T(1,128)} %param.8) | copy-start | bytes 98308
  516.2 55.6 %all-to-all-start.2 = ((f32[1,128,4096]{2,0,1:T(1,128)}), f32[1,128,4096]{2,0,1:T(1,128)S(1)}, u32[]{:S(2)}, u32[]{:S(2)}) async-start(f32[1,128,4096]{2,0,1:T(1,128)} %reshape_reshape_reshape.4), calls=%async_computation.2 | async-start | bytes 4194304 | tf_op jit(solution)/shard_map/all_to_all | solution.py:72
  541.8 739.2 %reduce-scatter.4.cloned.1.call-start = ((), (), s32[]{:S(2)}) async-start(), calls=%async_computation.5 | async-start | bytes 4227072
Sparse Core Ops, SparseCore 0:
  197.5 41.1 all-gather.1
  634.5 646.4 reduce-scatter.3
